TPU v7x, 32 devices: a whole 2x2x4 slice. The times are simulated.
32 devices in a mesh: depth: 2 (over core), freq: 16 (over z, y, x).
Axes of the slice: x: 2, y: 2, z: 4, core: 2. Of those that a mesh axis runs over, the one named last changes fastest.
Arguments:
- p_top: bfloat16 [16, 1024, 128], P('freq'), may hold values from -6 to 6
- upgoing: bfloat16 [2, 16, 1024, 128], P('depth', 'freq'), may hold values from -6 to 6
- extrapolator: bfloat16 [2, 16, 2, 1024, 1024], P('depth', 'freq'), may hold values from -0.125 to 0.125
- reflectivity: bfloat16 [2, 1024, 1024], P('depth', 'freq'), may hold values from -0.1875 to 0.1875
Outputs:
- wavefields: bfloat16 [2, 16, 1024, 128], P('depth', 'freq')
- images: float32 [2, 1024, 1024], P('depth', 'freq')
All inputs are finite; a program needn't handle non-finite values.
Results may differ from a plain program's by a relative error of at most 0.014.
Values may be sent and summed in bfloat16 or wider, within the bound.
No kernel may reach another device: no remote copies, remote signals or barrier semaphores. Data moves between devices by JAX's collectives and lax.ppermute only.
A program may use at most 64 MiB of HBM per device.

v0:
```python
import jax
import jax.numpy as jnp
from jax import lax
from jax.sharding import PartitionSpec as P


def shifted(value, axis, by):
    devices = lax.axis_size(axis)
    pairs = [(i, i + by) for i in range(devices) if 0 <= i + by < devices]
    return lax.ppermute(value, axis, pairs)


def extrapolate(real_w, imag_w, diff):
    half = diff.shape[-1] // 2
    first = jnp.dot(real_w, diff, preferred_element_type=jnp.float32)
    second = jnp.dot(imag_w, diff, preferred_element_type=jnp.float32)
    real_part = first[:, :half] - second[:, half:]
    imag_part = first[:, half:] + second[:, :half]
    return jnp.concatenate([real_part, imag_part], axis=1).astype(jnp.bfloat16)


def local(p_top, upgoing, extrapolator, reflectivity):
    upper = upgoing[0, 0]
    real_w = extrapolator[0, 0, 0]
    imag_w = extrapolator[0, 0, 1]
    top_field = p_top[0]
    columns = upper.shape[1]
    sections = lax.axis_size("depth")
    section = lax.axis_index("depth")
    is_first = section == 0
    rq_full = jnp.dot(
        lax.all_gather(reflectivity[0], "freq", axis=0, tiled=True),
        upper,
        preferred_element_type=jnp.float32,
    )

    def advance(incoming, rq_part):
        diff = (incoming.astype(jnp.float32) - rq_part).astype(jnp.bfloat16)
        return extrapolate(real_w, imag_w, diff)

    incoming = jnp.where(is_first, top_field, jnp.zeros_like(top_field))
    below = advance(incoming, rq_full)

    def whole_step(step, carry):
        inc_now, below_now = carry
        moved = shifted(below_now, "depth", 1)
        inc_next = jnp.where(is_first, top_field, moved)
        return (inc_next, advance(inc_next, rq_full))

    incoming, below = lax.fori_loop(0, sections - 1, whole_step, (incoming, below))
    scale = (float(columns) * lax.axis_size("freq")) ** (-0.5)
    picture = (
        lax.psum_scatter(
            lax.dot_general(
                upper, incoming, (((1,), (1,)), ((), ())), preferred_element_type=jnp.float32
            ),
            "freq",
            scatter_dimension=0,
            tiled=True,
        )
        * scale
    )
    return (below[None, None], picture[None])


def solution(mesh):
    in_specs = (
        P("freq", None, None),
        P("depth", "freq", None, None),
        P("depth", "freq", None, None, None),
        P("depth", "freq", None),
    )
    out_specs = (P("depth", "freq", None, None), P("depth", "freq", None))
    return jax.shard_map(local, mesh=mesh, in_specs=in_specs, out_specs=out_specs, check_vma=False)
```

profile of v0, /device:TPU:0, one launch (start us, length us, event | category | flops | bytes accessed | tf_op | source)
XLA Modules:
  0.0 193.5 jit_solution(11771704683910217558)
XLA Ops:
  7.2 0.0 copy-start
  7.2 0.0 all-gather.3.cloned.1.call-start
  7.2 0.7 all-gather.3.cloned.1.call-update
  7.9 0.0 reduce-scatter.4.cloned.1.call-start
  8.0 65.9 %all-gather.3.cloned.1.call-done = bf16[1,1024,1024]{2,1,0:T(8,128)(2,1)} async-done(((bf16[1,64,1024]{2,1,0:T(8,128)(2,1)}), bf16[1,1024,1024]{2,1,0:T(8,128)(2,1)}) %all-gather.3.cloned.1.call-update) | async-done | bytes 2097168 | tf_op jit(solution)/shard_map/all_gather | solution.py:32
  73.9 0.0 copy-done
  73.9 0.0 copy-start.2
  73.9 2.5 %subtract_convert_fusion.1 = (bf16[1024,128]{1,0:T(8,128)(2,1)S(1)}, f32[1024,128]{1,0:T(8,128)S(1)}) fusion(bf16[1,1024,128]{2,1,0:T(8,128)(2,1)} %param.4, pred[]{:T(512)S(6)} %eq.3, bf16[1,1,1024,128]{3,2,1,0:T(8,128)(2,1)S(1)} %copy-done, bf16[1,1024,1024]{2,1,0:T(8,128)(2,1)} %all-gather.3.cloned.1.call-done), kind=kOutput, calls=%fused_computation.25 | convolution fusion | flops 268959744 | bytes 3407873 | tf_op jit(solution)/shard_map/dot_general | solution.py:31
  76.4 2.3 %fusion.14 = f32[1024,128]{1,0:T(8,128)S(1)} fusion(bf16[1024,128]{1,0:T(8,128)(2,1)S(1)} %get-tuple-element.33, bf16[1,1,2,1024,1024]{4,3,2,1,0:T(8,128)(2,1)} %param.6), kind=kOutput, calls=%fused_computation.15 | convolution fusion | flops 268435456 | bytes 2883584 | tf_op jit(solution)/shard_map/dot_general | solution.py:15
  78.6 0.0 copy-done.2
  78.7 0.0 copy-start.1
  78.7 0.7 fusion.20
  79.4 0.3 fusion.27
  79.7 0.1 pad_maximum_fusion
  79.9 1.3 collective-permute-start
  81.2 1.1 collective-permute-done
  82.3 0.0 copy-done.1
  82.3 2.7 %convolution_bitcast_fusion = f32[1024,1024]{0,1:T(8,128)} fusion(bf16[1,1,1024,128]{3,2,1,0:T(8,128)(2,1)S(1)} %copy-done, bf16[1024,128]{1,0:T(8,128)(2,1)S(1)} %collective-permute-done, bf16[1,1024,128]{2,1,0:T(8,128)(2,1)S(1)} %copy-done.1, pred[]{:T(512)S(6)} %eq.3), kind=kOutput, calls=%fused_computation | convolution fusion | flops 268566528 | bytes 4980737 | tf_op jit(solution)/shard_map/dot_general | solution.py:54
  85.0 5.4 %copy.16 = f32[1024,1024]{1,0:T(8,128)} copy(f32[1024,1024]{0,1:T(8,128)} %convolution_bitcast_fusion) | data formatting | bytes 8388608
  90.4 0.0 reduce-scatter.4.cloned.1.call-update
  90.4 0.0 copy-start.3
  90.4 0.1 subtract_convert_fusion
  90.5 2.6 %fusion.23 = f32[1024,128]{0,1:T(8,128)S(1)} fusion(bf16[1024,128]{1,0:T(8,128)(2,1)S(1)} %subtract_convert_fusion, bf16[1,1,2,1024,1024]{4,3,2,1,0:T(8,128)(2,1)} %param.6), kind=kOutput, calls=%fused_computation.18 | convolution fusion | flops 268435456 | bytes 2883584 | tf_op jit(solution)/shard_map/while/body/eval_jaxpr/dot_general | solution.py:16
  93.1 0.1 copy-done.3
  93.2 0.8 fusion.17
  94.1 0.1 fusion.32
  94.1 0.8 copy.12
  95.0 89.6 %reduce-scatter.4.cloned.1.call-done = f32[64,1024]{1,0:T(8,128)} async-done(((f32[1024,1024]{1,0:T(8,128)}), f32[64,1024]{1,0:T(8,128)}) %reduce-scatter.4.cloned.1.call-update) | async-done | bytes 262160
  184.6 1.1 copy.17
  185.8 0.9 copy.13
  (2 shorter events, 0.1 us)
Async XLA Ops:
  7.2 66.7 %copy-start = (bf16[1,1,1024,128]{3,2,1,0:T(8,128)(2,1)S(1)}, bf16[1,1,1024,128]{3,2,1,0:T(8,128)(2,1)}, u32[]{:S(2)}) copy-start(bf16[1,1,1024,128]{3,2,1,0:T(8,128)(2,1)} %param.5) | copy-start | bytes 786436
  7.2 66.7 %all-gather.3.cloned.1.call-start = ((), (), s32[]{:S(2)}) async-start(), calls=%async_computation.1 | async-start | bytes 2228224 | tf_op jit(solution)/shard_map/all_gather | solution.py:32
  7.9 176.7 %reduce-scatter.4.cloned.1.call-start = ((), (), s32[]{:S(2)}) async-start(), calls=%async_computation.2 | async-start | bytes 4456448
  73.9 4.8 %copy-start.2 = (bf16[1,1,2,1024,1024]{4,3,2,1,0:T(8,128)(2,1)S(1)}, bf16[1,1,2,1024,1024]{4,3,2,1,0:T(8,128)(2,1)}, u32[]{:S(2)}) copy-start(bf16[1,1,2,1024,1024]{4,3,2,1,0:T(8,128)(2,1)} %param.6) | copy-start | bytes 12582916
  78.7 3.7 %copy-start.1 = (bf16[1,1024,128]{2,1,0:T(8,128)(2,1)S(1)}, bf16[1,1024,128]{2,1,0:T(8,128)(2,1)}, u32[]{:S(2)}) copy-start(bf16[1,1024,128]{2,1,0:T(8,128)(2,1)} %param.4) | copy-start | bytes 786436
  79.9 2.4 %collective-permute-start = (bf16[1024,128]{1,0:T(8,128)(2,1)S(1)}, bf16[1024,128]{1,0:T(8,128)(2,1)S(1)}, u32[]{:S(2)}, u32[]{:S(2)}) collective-permute-start(bf16[1024,128]{1,0:T(8,128)(2,1)S(1)} %pad_maximum_fusion), channel_id=1, source_target_pairs={{0,16},{1,17},{2,18},{3,19},{4,20},{5,21},{6,22},{7,23},{8,24},{9,... | collective-permute-start | bytes 786440 | tf_op jit(solution)/shard_map/while/body/eval_jaxpr/ppermute | solution.py:10
  90.4 2.8 %copy-start.3 = (bf16[1,1,2,1024,1024]{4,3,2,1,0:T(8,128)(2,1)S(1)}, bf16[1,1,2,1024,1024]{4,3,2,1,0:T(8,128)(2,1)}, u32[]{:S(2)}) copy-start(bf16[1,1,2,1024,1024]{4,3,2,1,0:T(8,128)(2,1)} %param.6) | copy-start | bytes 12582916
Sparse Core Ops, SparseCore 0:
  10.8 63.0 all-gather.2
  90.5 94.0 reduce-scatter.3
where the time goes:
time: 194 us
  waiting for transfers between devices  157 us (81%)
  between operations  14.2 us (7%)
  matrix products  11.5 us (6%)
  local copies, waits for them, and re-layouts  8.39 us (4%)
    unnamed x3, waiting for transfers between devices  90.3 us
    all_gather x1, waiting for transfers between devices, local(): lax.all_gather(reflectivity[0], 'freq', axis=0, tiled=True)  65.9 us
    unnamed x12, local copies, waits for them, and re-layouts  8.39 us
  transfers between devices with their start and end apart: 3, of which 3 were waited for; matrix products, arithmetic and copies ran while one was open for 2% of the time, Pallas kernels for 0%

commit v1 on v0

--- a/solution.py
+++ b/solution.py
@@ -2,6 +2,27 @@
 import jax.numpy as jnp
 from jax import lax
 from jax.sharding import PartitionSpec as P
+
+
+def gather_around(value, axis, dim):
+    count, index, width = (lax.axis_size(axis), lax.axis_index(axis), value.shape[dim])
+    ahead = [(i, (i + 1) % count) for i in range(count)]
+    backward = [(i, (i - 1) % count) for i in range(count)]
+    filled = jnp.zeros((*value.shape[:dim], count * width, *value.shape[dim + 1 :]), value.dtype)
+    filled = lax.dynamic_update_slice_in_dim(filled, value, index * width, axis=dim)
+    from_left = from_right = value
+    middle = count // 2
+    for hop in range(1, middle + 1):
+        from_left = lax.ppermute(from_left, axis, ahead)
+        filled = lax.dynamic_update_slice_in_dim(
+            filled, from_left, (index - hop) % count * width, axis=dim
+        )
+        if hop < count - middle:
+            from_right = lax.ppermute(from_right, axis, backward)
+            filled = lax.dynamic_update_slice_in_dim(
+                filled, from_right, (index + hop) % count * width, axis=dim
+            )
+    return filled
 
 
 def shifted(value, axis, by):
@@ -29,9 +50,7 @@
     section = lax.axis_index("depth")
     is_first = section == 0
     rq_full = jnp.dot(
-        lax.all_gather(reflectivity[0], "freq", axis=0, tiled=True),
-        upper,
-        preferred_element_type=jnp.float32,
+        gather_around(reflectivity[0], "freq", 0), upper, preferred_element_type=jnp.float32
     )
 
     def advance(incoming, rq_part):

time: 194 us -> 194 us (level)
  starting transfers between devices: 1.38 us -> 42.4 us
  waiting for transfers between devices: 157 us -> 119 us
  matrix products: 11.5 us -> 8.23 us
    all_gather x1 -> x0, waiting for transfers between devices: 65.9 us -> none  [local(): lax.all_gather(reflectivity[0], 'freq', axis=0, tiled=True)]
    ppermute x0 -> x15, starting transfers between devices: none -> 41 us  [the longest x7 38 us: gather_around(): from_right = lax.ppermute(from_right, axis, backward)]
    ppermute x0 -> x15, waiting for transfers between devices: none -> 31.1 us  [the longest x8 30.9 us: gather_around(): from_left = lax.ppermute(from_left, axis, ahead)]
    unnamed x3 -> x2, waiting for transfers between devices: 90.3 us -> 86.8 us
    unnamed x12 -> x14, local copies, waits for them, and re-layouts: 8.39 us -> 8.55 us
  transfers between devices with their start and end apart: 3 -> 17, of which waited for: 3 -> 11; matrix products, arithmetic and copies ran while one was open for 2% -> 3% of each run, Pallas kernels for 0% -> 0%
where the time goes in v1:
time: 194 us
  waiting for transfers between devices  119 us (61%)
  starting transfers between devices  42.4 us (22%)
  between operations  14.3 us (7%)
  local copies, waits for them, and re-layouts  9.03 us (5%)
  matrix products  8.23 us (4%)
    unnamed x2, waiting for transfers between devices  86.8 us
    ppermute x7, starting transfers between devices, gather_around(): from_right = lax.ppermute(from_right, axis, backward)  38 us
    ppermute x8, waiting for transfers between devices, gather_around(): from_left = lax.ppermute(from_left, axis, ahead)  30.9 us
    unnamed x14, local copies, waits for them, and re-layouts  8.55 us
  transfers between devices with their start and end apart: 17, of which 11 were waited for; matrix products, arithmetic and copies ran while one was open for 3% of the time, Pallas kernels for 0%

profile of v1, /device:TPU:0, one launch (start us, length us, event | category | flops | bytes accessed | tf_op | source)
XLA Modules:
  0.0 193.7 jit_solution(2871736544163685466)
XLA Ops:
  7.2 0.0 copy-start
  7.2 0.0 reduce-scatter.4.cloned.1.call-start
  7.2 3.0 %collective-permute-start = (bf16[64,1024]{1,0:T(8,128)(2,1)}, bf16[64,1024]{1,0:T(8,128)(2,1)S(1)}, u32[]{:S(2)}, u32[]{:S(2)}) collective-permute-start(bf16[64,1024]{1,0:T(8,128)(2,1)} %bitcast.57), channel_id=1, source_target_pairs={{0,1},{1,2},{2,3},{3,4},{4,5},{5,6},{6,7},{7,8},{8,9},{9,10},{10,1... | collective-permute-start | bytes 393224 | tf_op jit(solution)/shard_map/ppermute | solution.py:16
  10.3 4.1 %collective-permute-start.1 = (bf16[64,1024]{1,0:T(8,128)(2,1)}, bf16[64,1024]{1,0:T(8,128)(2,1)S(1)}, u32[]{:S(2)}, u32[]{:S(2)}) collective-permute-start(bf16[64,1024]{1,0:T(8,128)(2,1)} %bitcast.58), channel_id=1, source_target_pairs={{0,15},{1,0},{2,1},{3,2},{4,3},{5,4},{6,5},{7,6},{8,7},{9,8},{10,9... | collective-permute-start | bytes 393224 | tf_op jit(solution)/shard_map/ppermute | solution.py:21
  14.3 0.3 broadcast_in_dim.11
  14.6 0.0 copy-start.1
  14.6 3.4 %collective-permute-done = bf16[64,1024]{1,0:T(8,128)(2,1)S(1)} collective-permute-done((bf16[64,1024]{1,0:T(8,128)(2,1)}, bf16[64,1024]{1,0:T(8,128)(2,1)S(1)}, u32[]{:S(2)}, u32[]{:S(2)}) %collective-permute-start) | collective-permute-done | bytes 131104 | tf_op jit(solution)/shard_map/ppermute | solution.py:16
  18.1 0.0 collective-permute-start.2
  18.1 0.2 collective-permute-done.1
  18.3 5.4 %collective-permute-start.3 = (bf16[64,1024]{1,0:T(8,128)(2,1)S(1)}, bf16[64,1024]{1,0:T(8,128)(2,1)S(1)}, u32[]{:S(2)}, u32[]{:S(2)}) collective-permute-start(bf16[64,1024]{1,0:T(8,128)(2,1)S(1)} %collective-permute-done.1), channel_id=1, source_target_pairs={{0,15},{1,0},{2,1},{3,2},{4,3},{5,4},{6,5},{7,6},{8,7},{9,8},{10,9... | collective-permute-start | bytes 393224 | tf_op jit(solution)/shard_map/ppermute | solution.py:21
  23.7 2.9 %collective-permute-done.2 = bf16[64,1024]{1,0:T(8,128)(2,1)S(1)} collective-permute-done((bf16[64,1024]{1,0:T(8,128)(2,1)S(1)}, bf16[64,1024]{1,0:T(8,128)(2,1)S(1)}, u32[]{:S(2)}, u32[]{:S(2)}) %collective-permute-start.2) | collective-permute-done | bytes 131104 | tf_op jit(solution)/shard_map/ppermute | solution.py:16
  26.6 5.7 %collective-permute-start.5 = (bf16[64,1024]{1,0:T(8,128)(2,1)S(1)}, bf16[64,1024]{1,0:T(8,128)(2,1)S(1)}, u32[]{:S(2)}, u32[]{:S(2)}) collective-permute-start(bf16[64,1024]{1,0:T(8,128)(2,1)S(1)} %collective-permute-done.3), channel_id=1, source_target_pairs={{0,15},{1,0},{2,1},{3,2},{4,3},{5,4},{6,5},{7,6},{8,7},{9,8},{10,9... | collective-permute-start | bytes 393224 | tf_op jit(solution)/shard_map/ppermute | solution.py:21
  32.4 2.9 %collective-permute-done.4 = bf16[64,1024]{1,0:T(8,128)(2,1)S(1)} collective-permute-done((bf16[64,1024]{1,0:T(8,128)(2,1)S(1)}, bf16[64,1024]{1,0:T(8,128)(2,1)S(1)}, u32[]{:S(2)}, u32[]{:S(2)}) %collective-permute-start.4) | collective-permute-done | bytes 131104 | tf_op jit(solution)/shard_map/ppermute | solution.py:16
  35.3 0.0 collective-permute-start.6
  35.3 0.0 collective-permute-done.5
  35.3 5.7 %collective-permute-start.7 = (bf16[64,1024]{1,0:T(8,128)(2,1)S(1)}, bf16[64,1024]{1,0:T(8,128)(2,1)S(1)}, u32[]{:S(2)}, u32[]{:S(2)}) collective-permute-start(bf16[64,1024]{1,0:T(8,128)(2,1)S(1)} %collective-permute-done.5), channel_id=1, source_target_pairs={{0,15},{1,0},{2,1},{3,2},{4,3},{5,4},{6,5},{7,6},{8,7},{9,8},{10,9... | collective-permute-start | bytes 393224 | tf_op jit(solution)/shard_map/ppermute | solution.py:21
  41.1 2.9 %collective-permute-done.6 = bf16[64,1024]{1,0:T(8,128)(2,1)S(1)} collective-permute-done((bf16[64,1024]{1,0:T(8,128)(2,1)S(1)}, bf16[64,1024]{1,0:T(8,128)(2,1)S(1)}, u32[]{:S(2)}, u32[]{:S(2)}) %collective-permute-start.6) | collective-permute-done | bytes 131104 | tf_op jit(solution)/shard_map/ppermute | solution.py:16
  44.0 5.6 %collective-permute-start.9 = (bf16[64,1024]{1,0:T(8,128)(2,1)S(1)}, bf16[64,1024]{1,0:T(8,128)(2,1)S(1)}, u32[]{:S(2)}, u32[]{:S(2)}) collective-permute-start(bf16[64,1024]{1,0:T(8,128)(2,1)S(1)} %collective-permute-done.7), channel_id=1, source_target_pairs={{0,15},{1,0},{2,1},{3,2},{4,3},{5,4},{6,5},{7,6},{8,7},{9,8},{10,9... | collective-permute-start | bytes 393224 | tf_op jit(solution)/shard_map/ppermute | solution.py:21
  49.6 3.0 %collective-permute-done.8 = bf16[64,1024]{1,0:T(8,128)(2,1)S(1)} collective-permute-done((bf16[64,1024]{1,0:T(8,128)(2,1)S(1)}, bf16[64,1024]{1,0:T(8,128)(2,1)S(1)}, u32[]{:S(2)}, u32[]{:S(2)}) %collective-permute-start.8) | collective-permute-done | bytes 131104 | tf_op jit(solution)/shard_map/ppermute | solution.py:16
  52.6 0.0 collective-permute-done.9
  52.6 5.6 %collective-permute-start.11 = (bf16[64,1024]{1,0:T(8,128)(2,1)S(1)}, bf16[64,1024]{1,0:T(8,128)(2,1)S(1)}, u32[]{:S(2)}, u32[]{:S(2)}) collective-permute-start(bf16[64,1024]{1,0:T(8,128)(2,1)S(1)} %collective-permute-done.9), channel_id=1, source_target_pairs={{0,15},{1,0},{2,1},{3,2},{4,3},{5,4},{6,5},{7,6},{8,7},{9,8},{10,9... | collective-permute-start | bytes 393224 | tf_op jit(solution)/shard_map/ppermute | solution.py:21
  58.3 3.2 %collective-permute-done.10 = bf16[64,1024]{1,0:T(8,128)(2,1)S(1)} collective-permute-done((bf16[64,1024]{1,0:T(8,128)(2,1)S(1)}, bf16[64,1024]{1,0:T(8,128)(2,1)S(1)}, u32[]{:S(2)}, u32[]{:S(2)}) %collective-permute-start.10) | collective-permute-done | bytes 131104 | tf_op jit(solution)/shard_map/ppermute | solution.py:16
  61.5 5.9 %collective-permute-start.13 = (bf16[64,1024]{1,0:T(8,128)(2,1)S(1)}, bf16[64,1024]{1,0:T(8,128)(2,1)S(1)}, u32[]{:S(2)}, u32[]{:S(2)}) collective-permute-start(bf16[64,1024]{1,0:T(8,128)(2,1)S(1)} %collective-permute-done.11), channel_id=1, source_target_pairs={{0,15},{1,0},{2,1},{3,2},{4,3},{5,4},{6,5},{7,6},{8,7},{9,8},{10,9... | collective-permute-start | bytes 393224 | tf_op jit(solution)/shard_map/ppermute | solution.py:21
  67.5 0.0 copy-start.3
  67.5 4.0 %collective-permute-done.12 = bf16[64,1024]{1,0:T(8,128)(2,1)S(1)} collective-permute-done((bf16[64,1024]{1,0:T(8,128)(2,1)S(1)}, bf16[64,1024]{1,0:T(8,128)(2,1)S(1)}, u32[]{:S(2)}, u32[]{:S(2)}) %collective-permute-start.12) | collective-permute-done | bytes 131104 | tf_op jit(solution)/shard_map/ppermute | solution.py:16
  71.5 0.0 collective-permute-start.14
  71.5 0.0 collective-permute-done.13
  71.5 8.5 %collective-permute-done.14 = bf16[64,1024]{1,0:T(8,128)(2,1)S(1)} collective-permute-done((bf16[64,1024]{1,0:T(8,128)(2,1)S(1)}, bf16[64,1024]{1,0:T(8,128)(2,1)S(1)}, u32[]{:S(2)}, u32[]{:S(2)}) %collective-permute-start.14) | collective-permute-done | bytes 131104 | tf_op jit(solution)/shard_map/ppermute | solution.py:16
  80.1 0.7 subtract_convert_fusion.1
  80.8 0.7 fusion.12
  81.5 0.7 fusion.18
  82.2 0.3 fusion.25
  82.6 0.1 pad_maximum_fusion
  82.7 1.3 collective-permute-start.15
  84.0 1.1 collective-permute-done.15
  85.2 2.7 %convolution_bitcast_fusion = f32[1024,1024]{0,1:T(8,128)} fusion(bf16[1,1,1024,128]{3,2,1,0:T(8,128)(2,1)S(1)} %copy-done, bf16[1024,128]{1,0:T(8,128)(2,1)S(1)} %collective-permute-done.15, bf16[1,1024,128]{2,1,0:T(8,128)(2,1)S(1)} %copy-done.1, pred[]{:T(512)S(6)} %eq.19), kind=kOutput, calls=%fused_computation | convolution fusion | flops 268566528 | bytes 4980737 | tf_op jit(solution)/shard_map/dot_general | solution.py:73
  87.9 5.3 %copy.16 = f32[1024,1024]{1,0:T(8,128)} copy(f32[1024,1024]{0,1:T(8,128)} %convolution_bitcast_fusion) | data formatting | bytes 8388608
  93.2 0.0 reduce-scatter.4.cloned.1.call-update
  93.2 0.0 copy-start.4
  93.2 0.1 subtract_convert_fusion
  93.3 2.6 %fusion.21 = f32[1024,128]{0,1:T(8,128)S(1)} fusion(bf16[1024,128]{1,0:T(8,128)(2,1)S(1)} %subtract_convert_fusion, bf16[1,1,2,1024,1024]{4,3,2,1,0:T(8,128)(2,1)} %param.6), kind=kOutput, calls=%fused_computation.16 | convolution fusion | flops 268435456 | bytes 2883584 | tf_op jit(solution)/shard_map/while/body/eval_jaxpr/dot_general | solution.py:37
  95.9 0.3 copy-done.4
  96.2 0.8 fusion.15
  97.1 0.1 fusion.31
  97.2 0.8 copy.12
  98.0 86.8 %reduce-scatter.4.cloned.1.call-done = f32[64,1024]{1,0:T(8,128)} async-done(((f32[1024,1024]{1,0:T(8,128)}), f32[64,1024]{1,0:T(8,128)}) %reduce-scatter.4.cloned.1.call-update) | async-done | bytes 262160
  184.8 1.1 copy.17
  186.0 0.9 copy.13
  (30 shorter events, 0.3 us)
Async XLA Ops:
  7.2 72.9 %copy-start = (bf16[1,1,1024,128]{3,2,1,0:T(8,128)(2,1)S(1)}, bf16[1,1,1024,128]{3,2,1,0:T(8,128)(2,1)}, u32[]{:S(2)}) copy-start(bf16[1,1,1024,128]{3,2,1,0:T(8,128)(2,1)} %param.5) | copy-start | bytes 786436
  7.2 7.4 %copy-start.2 = (bf16[1,64,1024]{2,1,0:T(8,128)(2,1)S(1)}, bf16[1,64,1024]{2,1,0:T(8,128)(2,1)}, u32[]{:S(2)}) copy-start(bf16[1,64,1024]{2,1,0:T(8,128)(2,1)} %param.7) | copy-start | bytes 393220
  7.2 177.6 %reduce-scatter.4.cloned.1.call-start = ((), (), s32[]{:S(2)}) async-start(), calls=%async_computation.1 | async-start | bytes 4456448
  7.2 10.8 %collective-permute-start = (bf16[64,1024]{1,0:T(8,128)(2,1)}, bf16[64,1024]{1,0:T(8,128)(2,1)S(1)}, u32[]{:S(2)}, u32[]{:S(2)}) collective-permute-start(bf16[64,1024]{1,0:T(8,128)(2,1)} %bitcast.57), channel_id=1, source_target_pairs={{0,1},{1,2},{2,3},{3,4},{4,5},{5,6},{6,7},{7,8},{8,9},{9,10},{10,1... | collective-permute-start | bytes 393224 | tf_op jit(solution)/shard_map/ppermute | solution.py:16
  10.3 8.1 %collective-permute-start.1 = (bf16[64,1024]{1,0:T(8,128)(2,1)}, bf16[64,1024]{1,0:T(8,128)(2,1)S(1)}, u32[]{:S(2)}, u32[]{:S(2)}) collective-permute-start(bf16[64,1024]{1,0:T(8,128)(2,1)} %bitcast.58), channel_id=1, source_target_pairs={{0,15},{1,0},{2,1},{3,2},{4,3},{5,4},{6,5},{7,6},{8,7},{9,8},{10,9... | collective-permute-start | bytes 393224 | tf_op jit(solution)/shard_map/ppermute | solution.py:21
  14.6 65.5 %copy-start.1 = (bf16[1,1024,128]{2,1,0:T(8,128)(2,1)S(1)}, bf16[1,1024,128]{2,1,0:T(8,128)(2,1)}, u32[]{:S(2)}) copy-start(bf16[1,1024,128]{2,1,0:T(8,128)(2,1)} %param.4) | copy-start | bytes 786436
  18.1 8.6 %collective-permute-start.2 = (bf16[64,1024]{1,0:T(8,128)(2,1)S(1)}, bf16[64,1024]{1,0:T(8,128)(2,1)S(1)}, u32[]{:S(2)}, u32[]{:S(2)}) collective-permute-start(bf16[64,1024]{1,0:T(8,128)(2,1)S(1)} %collective-permute-done), channel_id=1, source_target_pairs={{0,1},{1,2},{2,3},{3,4},{4,5},{5,6},{6,7},{7,8},{8,9},{9,10},{10,1... | collective-permute-start | bytes 393224 | tf_op jit(solution)/shard_map/ppermute | solution.py:16
  18.3 8.3 %collective-permute-start.3 = (bf16[64,1024]{1,0:T(8,128)(2,1)S(1)}, bf16[64,1024]{1,0:T(8,128)(2,1)S(1)}, u32[]{:S(2)}, u32[]{:S(2)}) collective-permute-start(bf16[64,1024]{1,0:T(8,128)(2,1)S(1)} %collective-permute-done.1), channel_id=1, source_target_pairs={{0,15},{1,0},{2,1},{3,2},{4,3},{5,4},{6,5},{7,6},{8,7},{9,8},{10,9... | collective-permute-start | bytes 393224 | tf_op jit(solution)/shard_map/ppermute | solution.py:21
  26.6 8.7 %collective-permute-start.4 = (bf16[64,1024]{1,0:T(8,128)(2,1)S(1)}, bf16[64,1024]{1,0:T(8,128)(2,1)S(1)}, u32[]{:S(2)}, u32[]{:S(2)}) collective-permute-start(bf16[64,1024]{1,0:T(8,128)(2,1)S(1)} %collective-permute-done.2), channel_id=1, source_target_pairs={{0,1},{1,2},{2,3},{3,4},{4,5},{5,6},{6,7},{7,8},{8,9},{9,10},{10,1... | collective-permute-start | bytes 393224 | tf_op jit(solution)/shard_map/ppermute | solution.py:16
  26.6 8.7 %collective-permute-start.5 = (bf16[64,1024]{1,0:T(8,128)(2,1)S(1)}, bf16[64,1024]{1,0:T(8,128)(2,1)S(1)}, u32[]{:S(2)}, u32[]{:S(2)}) collective-permute-start(bf16[64,1024]{1,0:T(8,128)(2,1)S(1)} %collective-permute-done.3), channel_id=1, source_target_pairs={{0,15},{1,0},{2,1},{3,2},{4,3},{5,4},{6,5},{7,6},{8,7},{9,8},{10,9... | collective-permute-start | bytes 393224 | tf_op jit(solution)/shard_map/ppermute | solution.py:21
  35.3 8.7 %collective-permute-start.6 = (bf16[64,1024]{1,0:T(8,128)(2,1)S(1)}, bf16[64,1024]{1,0:T(8,128)(2,1)S(1)}, u32[]{:S(2)}, u32[]{:S(2)}) collective-permute-start(bf16[64,1024]{1,0:T(8,128)(2,1)S(1)} %collective-permute-done.4), channel_id=1, source_target_pairs={{0,1},{1,2},{2,3},{3,4},{4,5},{5,6},{6,7},{7,8},{8,9},{9,10},{10,1... | collective-permute-start | bytes 393224 | tf_op jit(solution)/shard_map/ppermute | solution.py:16
  35.3 8.7 %collective-permute-start.7 = (bf16[64,1024]{1,0:T(8,128)(2,1)S(1)}, bf16[64,1024]{1,0:T(8,128)(2,1)S(1)}, u32[]{:S(2)}, u32[]{:S(2)}) collective-permute-start(bf16[64,1024]{1,0:T(8,128)(2,1)S(1)} %collective-permute-done.5), channel_id=1, source_target_pairs={{0,15},{1,0},{2,1},{3,2},{4,3},{5,4},{6,5},{7,6},{8,7},{9,8},{10,9... | collective-permute-start | bytes 393224 | tf_op jit(solution)/shard_map/ppermute | solution.py:21
  44.0 8.7 %collective-permute-start.8 = (bf16[64,1024]{1,0:T(8,128)(2,1)S(1)}, bf16[64,1024]{1,0:T(8,128)(2,1)S(1)}, u32[]{:S(2)}, u32[]{:S(2)}) collective-permute-start(bf16[64,1024]{1,0:T(8,128)(2,1)S(1)} %collective-permute-done.6), channel_id=1, source_target_pairs={{0,1},{1,2},{2,3},{3,4},{4,5},{5,6},{6,7},{7,8},{8,9},{9,10},{10,1... | collective-permute-start | bytes 393224 | tf_op jit(solution)/shard_map/ppermute | solution.py:16
  44.0 8.7 %collective-permute-start.9 = (bf16[64,1024]{1,0:T(8,128)(2,1)S(1)}, bf16[64,1024]{1,0:T(8,128)(2,1)S(1)}, u32[]{:S(2)}, u32[]{:S(2)}) collective-permute-start(bf16[64,1024]{1,0:T(8,128)(2,1)S(1)} %collective-permute-done.7), channel_id=1, source_target_pairs={{0,15},{1,0},{2,1},{3,2},{4,3},{5,4},{6,5},{7,6},{8,7},{9,8},{10,9... | collective-permute-start | bytes 393224 | tf_op jit(solution)/shard_map/ppermute | solution.py:21
  52.6 8.9 %collective-permute-start.10 = (bf16[64,1024]{1,0:T(8,128)(2,1)S(1)}, bf16[64,1024]{1,0:T(8,128)(2,1)S(1)}, u32[]{:S(2)}, u32[]{:S(2)}) collective-permute-start(bf16[64,1024]{1,0:T(8,128)(2,1)S(1)} %collective-permute-done.8), channel_id=1, source_target_pairs={{0,1},{1,2},{2,3},{3,4},{4,5},{5,6},{6,7},{7,8},{8,9},{9,10},{10,1... | collective-permute-start | bytes 393224 | tf_op jit(solution)/shard_map/ppermute | solution.py:16
  52.6 8.9 %collective-permute-start.11 = (bf16[64,1024]{1,0:T(8,128)(2,1)S(1)}, bf16[64,1024]{1,0:T(8,128)(2,1)S(1)}, u32[]{:S(2)}, u32[]{:S(2)}) collective-permute-start(bf16[64,1024]{1,0:T(8,128)(2,1)S(1)} %collective-permute-done.9), channel_id=1, source_target_pairs={{0,15},{1,0},{2,1},{3,2},{4,3},{5,4},{6,5},{7,6},{8,7},{9,8},{10,9... | collective-permute-start | bytes 393224 | tf_op jit(solution)/shard_map/ppermute | solution.py:21
  61.5 9.9 %collective-permute-start.12 = (bf16[64,1024]{1,0:T(8,128)(2,1)S(1)}, bf16[64,1024]{1,0:T(8,128)(2,1)S(1)}, u32[]{:S(2)}, u32[]{:S(2)}) collective-permute-start(bf16[64,1024]{1,0:T(8,128)(2,1)S(1)} %collective-permute-done.10), channel_id=1, source_target_pairs={{0,1},{1,2},{2,3},{3,4},{4,5},{5,6},{6,7},{7,8},{8,9},{9,10},{10,1... | collective-permute-start | bytes 393224 | tf_op jit(solution)/shard_map/ppermute | solution.py:16
  61.5 10.0 %collective-permute-start.13 = (bf16[64,1024]{1,0:T(8,128)(2,1)S(1)}, bf16[64,1024]{1,0:T(8,128)(2,1)S(1)}, u32[]{:S(2)}, u32[]{:S(2)}) collective-permute-start(bf16[64,1024]{1,0:T(8,128)(2,1)S(1)} %collective-permute-done.11), channel_id=1, source_target_pairs={{0,15},{1,0},{2,1},{3,2},{4,3},{5,4},{6,5},{7,6},{8,7},{9,8},{10,9... | collective-permute-start | bytes 393224 | tf_op jit(solution)/shard_map/ppermute | solution.py:21
  67.5 13.3 %copy-start.3 = (bf16[1,1,2,1024,1024]{4,3,2,1,0:T(8,128)(2,1)S(1)}, bf16[1,1,2,1024,1024]{4,3,2,1,0:T(8,128)(2,1)}, u32[]{:S(2)}) copy-start(bf16[1,1,2,1024,1024]{4,3,2,1,0:T(8,128)(2,1)} %param.6) | copy-start | bytes 12582916
  71.5 8.6 %collective-permute-start.14 = (bf16[64,1024]{1,0:T(8,128)(2,1)S(1)}, bf16[64,1024]{1,0:T(8,128)(2,1)S(1)}, u32[]{:S(2)}, u32[]{:S(2)}) collective-permute-start(bf16[64,1024]{1,0:T(8,128)(2,1)S(1)} %collective-permute-done.12), channel_id=1, source_target_pairs={{0,1},{1,2},{2,3},{3,4},{4,5},{5,6},{6,7},{7,8},{8,9},{9,10},{10,1... | collective-permute-start | bytes 393224 | tf_op jit(solution)/shard_map/ppermute | solution.py:16
  82.7 2.4 %collective-permute-start.15 = (bf16[1024,128]{1,0:T(8,128)(2,1)S(1)}, bf16[1024,128]{1,0:T(8,128)(2,1)S(1)}, u32[]{:S(2)}, u32[]{:S(2)}) collective-permute-start(bf16[1024,128]{1,0:T(8,128)(2,1)S(1)} %pad_maximum_fusion), channel_id=1, source_target_pairs={{0,16},{1,17},{2,18},{3,19},{4,20},{5,21},{6,22},{7,23},{8,24},{9,... | collective-permute-start | bytes 786440 | tf_op jit(solution)/shard_map/while/body/eval_jaxpr/ppermute | solution.py:31
  93.2 3.0 %copy-start.4 = (bf16[1,1,2,1024,1024]{4,3,2,1,0:T(8,128)(2,1)S(1)}, bf16[1,1,2,1024,1024]{4,3,2,1,0:T(8,128)(2,1)}, u32[]{:S(2)}) copy-start(bf16[1,1,2,1024,1024]{4,3,2,1,0:T(8,128)(2,1)} %param.6) | copy-start | bytes 12582916
Sparse Core Ops, SparseCore 0:
  93.4 91.3 reduce-scatter.3
